TPU v7x, 32 devices: a whole 2x2x4 slice. The times are simulated.
32 devices in a mesh: mode: 8 (over z, y), tm: 4 (over x, core).
Axes of the slice: x: 2, y: 2, z: 4, core: 2. Of those that a mesh axis runs over, the one named last changes fastest.
Arguments:
- support_accel: bfloat16 [512, 2048], P(None, 'tm'), may hold values from -6 to 6
- participation: bfloat16 [2048, 512], P('mode'), may hold values from -0.25 to 0.25
- kernels: float32 [2048, 2048], P('mode'), may hold values from -0.25 to 0.25
- lengths: int32 [2048], P('mode'), may hold values from 1 to 2048, as said below
- mode_shapes: bfloat16 [16384, 2048], P('mode'), may hold values from -0.125 to 0.125
- groups: int32 [16384], P('mode'), may hold values from 0 to 511
Outputs:
- response: bfloat16 [16384, 2048], P('mode', 'tm')
Inputs may be any that keep to these rules, and one draw needn't show every extreme that they name: `lengths`: some mode has exactly 2048 taps in every draw.
All inputs are finite; a program needn't handle non-finite values.
Results may differ from a plain program's by a relative error of at most 0.0033.
Values may be sent and summed in bfloat16 or wider, within the bound.
A program may use at most 64 MiB of HBM per device.

v0:
```python
import jax
import jax.numpy as jnp
from jax import lax
from jax.sharding import PartitionSpec as P


def passed_along(block, axis, distance):
    devices = range(lax.axis_size(axis))
    route = [(i - distance, i) for i in devices if i - distance in devices]
    return lax.ppermute(block, axis, route)


def depthwise(signal, weights):
    flipped = jnp.flip(weights, 1)[:, None, :]
    result = lax.conv_general_dilated(
        signal[None],
        flipped,
        (1,),
        "VALID",
        dimension_numbers=("NCH", "OIH", "NCH"),
        feature_group_count=signal.shape[0],
        precision=lax.Precision.HIGHEST,
    )
    return result[0]


def apply_filter(signal, kernel):
    return depthwise(signal, kernel)


def per_device(support_accel, participation, kernels, lengths, mode_shapes, groups):
    slab_len = support_accel.shape[1]
    tap_count = kernels.shape[1]
    depth_slabs = tap_count // slab_len
    forces = jnp.dot(participation, support_accel, preferred_element_type=jnp.float32)
    alive = jnp.arange(tap_count, dtype=jnp.int32)[None, :] < lengths[:, None]
    masked = jnp.where(alive, kernels, jnp.zeros_like(kernels))
    pieces = [forces]
    for distance in range(1, depth_slabs + 1):
        pieces.insert(0, passed_along(forces, "tm", distance))
    window = jnp.concatenate(pieces, axis=1)
    modal = apply_filter(window[:, 1:], masked).astype(jnp.bfloat16)
    initial = jnp.zeros((mode_shapes.shape[0], slab_len), jnp.float32)
    piece = jax.tree.map(lambda part: lax.all_gather(part, "mode", axis=0, tiled=True), modal)
    columns = lax.slice_in_dim(mode_shapes, 0, piece.shape[0], axis=1)
    summed = initial + jnp.dot(columns, piece, preferred_element_type=jnp.float32)
    ground = jnp.take(support_accel, groups, axis=0).astype(jnp.float32)
    return (summed + ground).astype(jnp.bfloat16)


def solution(mesh):
    placed = (
        P(None, "tm"),
        P("mode", None),
        P("mode", None),
        P("mode"),
        P("mode", None),
        P("mode"),
    )
    return jax.shard_map(
        per_device, mesh=mesh, in_specs=placed, out_specs=P("mode", "tm"), check_vma=False
    )
```

profile of v0, /device:TPU:0, one launch (start us, length us, event | category | flops | bytes accessed | tf_op | source)
XLA Modules:
  0.0 271.4 jit_solution(18268262673586640301)
XLA Ops:
  6.5 0.0 copy-start
  6.5 0.0 all-gather.3.cloned.1.call-start
  6.5 1.0 copy-done
  7.6 1.2 fusion.4
  8.8 1.5 collective-permute-start
  10.3 5.1 %collective-permute-start.1 = (f32[256,512]{1,0:T(8,128)S(1)}, f32[256,512]{1,0:T(8,128)}, u32[]{:S(2)}, u32[]{:S(2)}) collective-permute-start(f32[256,512]{1,0:T(8,128)S(1)} %fusion.4), channel_id=1, source_target_pairs={{0,3},{4,7},{8,11},{12,15},{16,19},{20,23},{24,27},{28,31}} | collective-permute-start | bytes 1572872 | tf_op jit(solution)/shard_map/ppermute | solution.py:10
  15.4 2.1 collective-permute-start.2
  17.5 2.1 collective-permute-start.3
  19.6 1.8 fusion.2
  21.4 11.6 %rev.4 = f32[256,2048]{1,0:T(8,128)} reverse(f32[256,2048]{1,0:T(8,128)S(1)} %fusion.2), dimensions={1} | reverse | bytes 4194304 | tf_op jit(solution)/shard_map/jit(_flip)/rev | solution.py:14
  33.0 6.1 %copy.12 = f32[256,1,2048]{0,1,2:T(1,128)} copy(f32[256,1,2048]{2,0,1:T(8,128)} %bitcast.15) | data formatting | bytes 4194304 | tf_op jit(solution)/shard_map/broadcast_in_dim | solution.py:14
  39.1 0.0 collective-permute-done
  39.1 1.1 constant_dynamic-update-slice_fusion.4
  40.2 0.0 collective-permute-done.1
  40.2 1.1 constant_dynamic-update-slice_fusion.3
  41.3 0.0 collective-permute-done.2
  41.3 1.1 constant_dynamic-update-slice_fusion.2
  42.3 0.0 collective-permute-done.3
  42.4 1.1 constant_dynamic-update-slice_fusion.1
  43.5 0.8 slice_bitcast_fusion
  44.2 4.0 %copy.11 = f32[1,256,2559]{1,0,2:T(1,128)} copy(f32[1,256,2559]{2,1,0:T(8,128)S(1)} %slice_bitcast_fusion) | data formatting | bytes 5240832 | tf_op jit(solution)/shard_map/broadcast_in_dim | solution.py:16
  48.3 0.0 copy-start.1
  48.3 90.9 %convolution_convert_fusion = bf16[1,256,512]{1,0,2:T(2,128)(2,1)} fusion(f32[1,256,2559]{1,0,2:T(1,128)} %copy.11, f32[256,1,2048]{0,1,2:T(1,128)} %copy.12), kind=kOutput, calls=%fused_computation.7 | convolution fusion | flops 3221356544 | bytes 4979712 | tf_op jit(solution)/shard_map/conv_general_dilated | solution.py:15
  139.1 0.0 all-gather.3.cloned.1.call-update
  139.2 0.0 copy-done.1
  139.2 7.5 %gather_fusion = bf16[2048,512]{1,0:T(8,128)(2,1)S(1)} fusion(bf16[512,512]{1,0:T(8,128)(2,1)S(1)} %copy-done, s32[2048]{0:T(1024)S(1)} %fusion.3), kind=kCustom, calls=%fused_computation | custom fusion | bytes 4202496 | tf_op jit(solution)/shard_map/jit(_take)/gather | solution.py:47
  146.7 2.4 copy.14
  149.1 92.8 %all-gather.3.cloned.1.call-done = bf16[1,2048,512]{1,0,2:T(2,128)(2,1)} async-done(((bf16[1,256,512]{1,0,2:T(2,128)(2,1)}), bf16[1,2048,512]{1,0,2:T(2,128)(2,1)}) %all-gather.3.cloned.1.call-update) | async-done | bytes 2097168 | tf_op jit(solution)/shard_map/all_gather | solution.py:44
  241.9 9.0 %copy.13 = bf16[1,2048,512]{2,1,0:T(8,128)(2,1)S(1)} copy(bf16[1,2048,512]{1,0,2:T(2,128)(2,1)} %all-gather.3.cloned.1.call-done) | data formatting | bytes 4194304 | tf_op jit(solution)/shard_map/all_gather | solution.py:44
  250.9 9.7 %fusion = bf16[2048,512]{0,1:T(8,128)(2,1)} fusion(bf16[2048,2048]{1,0:T(8,128)(2,1)} %param.10, bf16[1,2048,512]{2,1,0:T(8,128)(2,1)S(1)} %copy.13, bf16[2048,512]{0,1:T(8,128)(2,1)} %copy.14, pred[2048]{0:T(1024)(128)(4,1)S(1)} %compare_and_fusion), kind=kOutput, calls=%fused_computation.2 | convolution fusion | flops 4299161600 | bytes 14682112 | tf_op jit(solution)/shard_map/dot_general | solution.py:46
  260.6 3.9 %copy.15 = bf16[2048,512]{1,0:T(8,128)(2,1)} copy(bf16[2048,512]{0,1:T(8,128)(2,1)} %fusion) | data formatting | bytes 4194304 | tf_op jit(solution)/shard_map/convert_element_type | solution.py:48
  (3 shorter events, 0.1 us)
Async XLA Ops:
  6.5 1.0 copy-start
  6.5 235.4 %all-gather.3.cloned.1.call-start = ((), (), s32[]{:S(2)}) async-start(), calls=%async_computation | async-start | bytes 4718592 | tf_op jit(solution)/shard_map/all_gather | solution.py:44
  8.8 30.3 %collective-permute-start = (f32[256,512]{1,0:T(8,128)S(1)}, f32[256,512]{1,0:T(8,128)}, u32[]{:S(2)}, u32[]{:S(2)}) collective-permute-start(f32[256,512]{1,0:T(8,128)S(1)} %fusion.4), channel_id=1, source_target_pairs={} | collective-permute-start | bytes 1572872 | tf_op jit(solution)/shard_map/ppermute | solution.py:10
  10.3 29.9 %collective-permute-start.1 = (f32[256,512]{1,0:T(8,128)S(1)}, f32[256,512]{1,0:T(8,128)}, u32[]{:S(2)}, u32[]{:S(2)}) collective-permute-start(f32[256,512]{1,0:T(8,128)S(1)} %fusion.4), channel_id=1, source_target_pairs={{0,3},{4,7},{8,11},{12,15},{16,19},{20,23},{24,27},{28,31}} | collective-permute-start | bytes 1572872 | tf_op jit(solution)/shard_map/ppermute | solution.py:10
  15.4 25.9 %collective-permute-start.2 = (f32[256,512]{1,0:T(8,128)S(1)}, f32[256,512]{1,0:T(8,128)}, u32[]{:S(2)}, u32[]{:S(2)}) collective-permute-start(f32[256,512]{1,0:T(8,128)S(1)} %fusion.4), channel_id=1, source_target_pairs={{0,2},{1,3},{4,6},{5,7},{8,10},{9,11},{12,14},{13,15},{16,18},{17,... | collective-permute-start | bytes 1572872 | tf_op jit(solution)/shard_map/ppermute | solution.py:10
  17.5 24.9 %collective-permute-start.3 = (f32[256,512]{1,0:T(8,128)S(1)}, f32[256,512]{1,0:T(8,128)}, u32[]{:S(2)}, u32[]{:S(2)}) collective-permute-start(f32[256,512]{1,0:T(8,128)S(1)} %fusion.4), channel_id=1, source_target_pairs={{0,1},{1,2},{2,3},{4,5},{5,6},{6,7},{8,9},{9,10},{10,11},{12,13},{... | collective-permute-start | bytes 1572872 | tf_op jit(solution)/shard_map/ppermute | solution.py:10
  48.3 90.9 %copy-start.1 = (s32[2048]{0:T(1024)S(1)}, s32[2048]{0:T(1024)}, u32[]{:S(2)}) copy-start(s32[2048]{0:T(1024)} %param.11) | copy-start | bytes 24580
Sparse Core Ops, SparseCore 0:
  139.3 102.5 all-gather.2
where the time goes:
time: 272 us; the launch traced here: 271 us
  matrix products  102 us (38%)
  waiting for transfers between devices  92.8 us (34%)
  local copies, waits for them, and re-layouts  50.7 us (19%)
  between operations  13.5 us (5%)
  starting transfers between devices  10.8 us (4%)
    all_gather x1, waiting for transfers between devices, per_device(): lax.all_gather(part, 'mode', axis=0, tiled=True)  92.8 us
    conv_general_dilated x1, matrix products, depthwise(): lax.conv_general_dilated(signal[None], flipped, (1,), 'VALID', dimension_...  90.9 us
    rev x1, local copies, waits for them, and re-layouts, depthwise(): flipped = jnp.flip(weights, 1)[:, None, :]  11.6 us
    ppermute x4, starting transfers between devices, passed_along(): return lax.ppermute(block, axis, route)  10.7 us
    gather x2, local copies, waits for them, and re-layouts, per_device(): ground = jnp.take(support_accel, groups, axis=0).astype(jnp.float32)  9.92 us
    dot_general x1, matrix products, per_device(): jnp.dot(columns, piece, preferred_element_type=jnp.float32)  9.71 us
    all_gather x1, local copies, waits for them, and re-layouts, per_device(): lax.all_gather(part, 'mode', axis=0, tiled=True)  8.97 us
    broadcast_in_dim x1, local copies, waits for them, and re-layouts, depthwise(): flipped = jnp.flip(weights, 1)[:, None, :]  6.06 us
  transfers between devices with their start and end apart: 5, of which 1 were waited for; matrix products, arithmetic and copies ran while one was open for 12% of the time, Pallas kernels for 0%

commit v1 on v0

--- a/solution.py
+++ b/solution.py
@@ -1,7 +1,34 @@
+import functools
 import jax
 import jax.numpy as jnp
 from jax import lax
 from jax.sharding import PartitionSpec as P
+
+
+def name_inputs_all(array_in, axis_k):
+    array_in = jnp.moveaxis(array_in, 0, axis_k)
+    later = array_in.shape
+    return array_in.reshape(
+        *later[:axis_k], later[axis_k] * later[axis_k + 1], *later[axis_k + 2 :]
+    )
+
+
+def edit_heads_for(z_in, ax_name, join_dim):
+    dev_count = lax.axis_size(ax_name)
+    carry = range(dev_count)
+    base_arr = map(lambda p: (p, (p + 1) % dev_count), carry)
+    by_rank = list(base_arr)
+    rack = [z_in]
+    while len(rack) < dev_count:
+        ready = lax.ppermute(rack[-1], ax_name, by_rank)
+        rack.append(ready)
+    long_array = lax.axis_index(ax_name)
+    seen_now = jnp.stack(rack)
+    rack = seen_now[(long_array - jnp.arange(dev_count)) % dev_count]
+    return name_inputs_all(rack, join_dim)
+
+
+follow_the_notes = functools.partial(edit_heads_for, ax_name="mode", join_dim=0)
 
 
 def passed_along(block, axis, distance):
@@ -41,7 +68,7 @@
     window = jnp.concatenate(pieces, axis=1)
     modal = apply_filter(window[:, 1:], masked).astype(jnp.bfloat16)
     initial = jnp.zeros((mode_shapes.shape[0], slab_len), jnp.float32)
-    piece = jax.tree.map(lambda part: lax.all_gather(part, "mode", axis=0, tiled=True), modal)
+    piece = jax.tree.map(lambda part: follow_the_notes(part), modal)
     columns = lax.slice_in_dim(mode_shapes, 0, piece.shape[0], axis=1)
     summed = initial + jnp.dot(columns, piece, preferred_element_type=jnp.float32)
     ground = jnp.take(support_accel, groups, axis=0).astype(jnp.float32)

time: 272 us -> 244 us (0.90)
  waiting for transfers between devices: 92.8 us -> 56.3 us
  local copies, waits for them, and re-layouts: 50.7 us -> 71.7 us
  between operations: 13.5 us -> 0.15 us
    all_gather x1 -> x0, waiting for transfers between devices: 92.8 us -> none  [per_device(): lax.all_gather(part, 'mode', axis=0, tiled=True)]
    ppermute x0 -> x7, waiting for transfers between devices: none -> 56.3 us  [edit_heads_for(): ready = lax.ppermute(rack[-1], ax_name, by_rank)]
    another operation x0 -> x9, local copies, waits for them, and re-layouts: none -> 24.1 us  [edit_heads_for(): seen_now = jnp.stack(rack)]
    all_gather x1 -> x0, local copies, waits for them, and re-layouts: 8.97 us -> none  [per_device(): lax.all_gather(part, 'mode', axis=0, tiled=True)]
    gather x0 -> x1, local copies, waits for them, and re-layouts: none -> 3.73 us  [edit_heads_for(): rack = seen_now[(long_array - jnp.arange(dev_count)) % dev_count]]
    unnamed x8 -> x22, local copies, waits for them, and re-layouts: 5.35 us -> 6.8 us
  transfers between devices with their start and end apart: 5 -> 11, of which waited for: 1 -> 6; matrix products, arithmetic and copies ran while one was open for 12% -> 17% of each run, Pallas kernels for 0% -> 0%
where the time goes in v1:
time: 244 us; the launch traced here: 242 us
  matrix products  99.9 us (41%)
  local copies, waits for them, and re-layouts  71.7 us (29%)
  waiting for transfers between devices  56.3 us (23%)
  starting transfers between devices  12.4 us (5%)
    conv_general_dilated x1, matrix products, depthwise(): lax.conv_general_dilated(signal[None], flipped, (1,), 'VALID', dimension_...  88.7 us
    ppermute x7, waiting for transfers between devices, edit_heads_for(): ready = lax.ppermute(rack[-1], ax_name, by_rank)  56.3 us
    another operation x9, local copies, waits for them, and re-layouts, edit_heads_for(): seen_now = jnp.stack(rack)  24.1 us
    rev x1, local copies, waits for them, and re-layouts, depthwise(): flipped = jnp.flip(weights, 1)[:, None, :]  11.6 us
    ppermute x4, starting transfers between devices, passed_along(): return lax.ppermute(block, axis, route)  10.8 us
    gather x2, local copies, waits for them, and re-layouts, per_device(): ground = jnp.take(support_accel, groups, axis=0).astype(jnp.float32)  10 us
    dot_general x1, matrix products, per_device(): jnp.dot(columns, piece, preferred_element_type=jnp.float32)  9.92 us
    unnamed x22, local copies, waits for them, and re-layouts  6.8 us
  transfers between devices with their start and end apart: 11, of which 6 were waited for; matrix products, arithmetic and copies ran while one was open for 17% of the time, Pallas kernels for 0%

profile of v1, /device:TPU:0, one launch (start us, length us, event | category | flops | bytes accessed | tf_op | source)
XLA Modules:
  0.0 242.3 jit_solution(6021438504375579790)
XLA Ops:
  1.0 1.2 fusion.5
  2.3 1.5 collective-permute-start
  3.8 5.1 %collective-permute-start.1 = (f32[256,512]{1,0:T(8,128)S(1)}, f32[256,512]{1,0:T(8,128)}, u32[]{:S(2)}, u32[]{:S(2)}) collective-permute-start(f32[256,512]{1,0:T(8,128)S(1)} %fusion.5), channel_id=1, source_target_pairs={{0,3},{4,7},{8,11},{12,15},{16,19},{20,23},{24,27},{28,31}} | collective-permute-start | bytes 1572872 | tf_op jit(solution)/shard_map/ppermute | solution.py:37
  8.9 2.1 collective-permute-start.2
  11.0 2.1 collective-permute-start.3
  13.1 1.8 fusion.1
  14.9 11.6 %rev.4 = f32[256,2048]{1,0:T(8,128)} reverse(f32[256,2048]{1,0:T(8,128)S(1)} %fusion.1), dimensions={1} | reverse | bytes 4194304 | tf_op jit(solution)/shard_map/jit(_flip)/rev | solution.py:41
  26.5 6.0 %copy.117 = f32[256,1,2048]{0,1,2:T(1,128)} copy(f32[256,1,2048]{2,0,1:T(8,128)} %bitcast.24) | data formatting | bytes 4194304 | tf_op jit(solution)/shard_map/broadcast_in_dim | solution.py:41
  33.7 1.1 constant_dynamic-update-slice_fusion.3
  34.7 1.1 constant_dynamic-update-slice_fusion.2
  35.8 1.1 constant_dynamic-update-slice_fusion.1
  37.7 4.0 %copy.116 = f32[1,256,2559]{1,0,2:T(1,128)} copy(f32[1,256,2559]{2,1,0:T(8,128)S(1)} %slice_bitcast_fusion) | data formatting | bytes 5240832 | tf_op jit(solution)/shard_map/broadcast_in_dim | solution.py:43
  41.7 88.7 %convolution_convert_fusion = bf16[1,256,512]{1,0,2:T(2,128)(2,1)S(1)} fusion(f32[1,256,2559]{1,0,2:T(1,128)} %copy.116, f32[256,1,2048]{0,1,2:T(1,128)} %copy.117), kind=kOutput, calls=%fused_computation.7 | convolution fusion | flops 3221356544 | bytes 4979712 | tf_op jit(solution)/shard_map/conv_general_dilated | solution.py:42
  131.1 1.6 collective-permute-start.4
  132.7 8.6 %collective-permute-done.4 = bf16[256,512]{1,0:T(8,128)(2,1)S(1)} collective-permute-done((bf16[256,512]{1,0:T(8,128)(2,1)S(1)}, bf16[256,512]{1,0:T(8,128)(2,1)S(1)}, u32[]{:S(2)}, u32[]{:S(2)}) %collective-permute-start.4) | collective-permute-done | bytes 262176 | tf_op jit(solution)/shard_map/ppermute | solution.py:23
  141.4 9.3 %collective-permute-done.5 = bf16[256,512]{1,0:T(8,128)(2,1)S(1)} collective-permute-done((bf16[256,512]{1,0:T(8,128)(2,1)S(1)}, bf16[256,512]{1,0:T(8,128)(2,1)S(1)}, u32[]{:S(2)}, u32[]{:S(2)}) %collective-permute-start.5) | collective-permute-done | bytes 262176 | tf_op jit(solution)/shard_map/ppermute | solution.py:23
  151.4 9.1 %collective-permute-done.6 = bf16[256,512]{1,0:T(8,128)(2,1)S(1)} collective-permute-done((bf16[256,512]{1,0:T(8,128)(2,1)S(1)}, bf16[256,512]{1,0:T(8,128)(2,1)S(1)}, u32[]{:S(2)}, u32[]{:S(2)}) %collective-permute-start.6) | collective-permute-done | bytes 262176 | tf_op jit(solution)/shard_map/ppermute | solution.py:23
  161.2 9.1 %collective-permute-done.7 = bf16[256,512]{1,0:T(8,128)(2,1)S(1)} collective-permute-done((bf16[256,512]{1,0:T(8,128)(2,1)S(1)}, bf16[256,512]{1,0:T(8,128)(2,1)S(1)}, u32[]{:S(2)}, u32[]{:S(2)}) %collective-permute-start.7) | collective-permute-done | bytes 262176 | tf_op jit(solution)/shard_map/ppermute | solution.py:23
  170.2 9.7 %collective-permute-done.8 = bf16[256,512]{1,0:T(8,128)(2,1)S(1)} collective-permute-done((bf16[256,512]{1,0:T(8,128)(2,1)S(1)}, bf16[256,512]{1,0:T(8,128)(2,1)S(1)}, u32[]{:S(2)}, u32[]{:S(2)}) %collective-permute-start.8) | collective-permute-done | bytes 262176 | tf_op jit(solution)/shard_map/ppermute | solution.py:23
  180.0 10.6 %collective-permute-done.9 = bf16[256,512]{1,0:T(8,128)(2,1)} collective-permute-done((bf16[256,512]{1,0:T(8,128)(2,1)S(1)}, bf16[256,512]{1,0:T(8,128)(2,1)}, u32[]{:S(2)}, u32[]{:S(2)}) %collective-permute-start.9) | collective-permute-done | bytes 262176 | tf_op jit(solution)/shard_map/ppermute | solution.py:23
  190.6 7.5 %gather_fusion.1 = bf16[2048,512]{1,0:T(8,128)(2,1)S(1)} fusion(bf16[512,512]{1,0:T(8,128)(2,1)S(1)} %copy-done, s32[2048]{0:T(1024)S(1)} %fusion.2), kind=kCustom, calls=%fused_computation.1 | custom fusion | bytes 4202496 | tf_op jit(solution)/shard_map/jit(_take)/gather | solution.py:74
  198.1 2.5 %copy.127 = bf16[2048,512]{0,1:T(8,128)(2,1)} copy(bf16[2048,512]{1,0:T(8,128)(2,1)S(1)} %gather_fusion.1) | data formatting | bytes 4194304 | tf_op jit(solution)/shard_map/jit(_take)/gather | solution.py:74
  200.6 1.1 copy.119
  201.7 1.9 copy.120
  203.6 1.9 copy.121
  207.7 2.0 copy.124
  209.7 1.9 copy.125
  211.6 10.4 %stack.32 = bf16[8,256,512]{1,0,2:T(8,128)(2,1)S(1)} concatenate(bf16[1,256,512]{1,0,2:T(2,128)(2,1)S(1)} %convolution_convert_fusion, bf16[1,256,512]{1,0,2:T(2,128)(2,1)} %copy.119, bf16[1,256,512]{1,0,2:T(2,128)(2,1)} %copy.120, bf16[1,256,512]{1,0,2:T(2,128)(2,1)} %copy.121, bf16[1,256,512]{1,0,2:T(2,128)(2,1)} %copy.122, bf16[1,256,512]{1,0,2:T(2,128)(2,1)} %copy.123, ...), dimensions={0} | concatenate | bytes 4194304 | tf_op jit(solution)/shard_map/stack | solution.py:26
  222.0 2.7 %copy.126 = bf16[8,256,512]{2,1,0:T(8,128)(2,1)} copy(bf16[8,256,512]{1,0,2:T(8,128)(2,1)S(1)} %stack.32) | data formatting | bytes 4194304 | tf_op jit(solution)/shard_map/stack | solution.py:26
  224.7 3.7 %gather_fusion = bf16[8,256,512]{2,1,0:T(8,128)(2,1)} fusion(bf16[8,256,512]{2,1,0:T(8,128)(2,1)} %copy.126, s32[1024]{0:T(1024)S(1)} %pad_clamp_fusion), kind=kCustom, calls=%fused_computation | custom fusion | bytes 4194336 | tf_op jit(solution)/shard_map/gather | solution.py:27
  228.4 9.9 %fusion = bf16[2048,512]{0,1:T(8,128)(2,1)} fusion(bf16[2048,512]{1,0:T(8,128)(2,1)} %bitcast.25, bf16[2048,2048]{1,0:T(8,128)(2,1)} %param.10, bf16[2048,512]{0,1:T(8,128)(2,1)S(1)} %copy-done.1, pred[2048]{0:T(1024)(128)(4,1)S(1)} %compare_and_fusion), kind=kOutput, calls=%fused_computation.3 | convolution fusion | flops 4299161600 | bytes 14682112 | tf_op jit(solution)/shard_map/dot_general | solution.py:73
  238.4 3.9 %copy.128 = bf16[2048,512]{1,0:T(8,128)(2,1)} copy(bf16[2048,512]{0,1:T(8,128)(2,1)} %fusion) | data formatting | bytes 4194304 | tf_op jit(solution)/shard_map/convert_element_type | solution.py:75
  (39 shorter events, 7.2 us)
Async XLA Ops:
  0.0 1.0 copy-start
  2.3 30.3 %collective-permute-start = (f32[256,512]{1,0:T(8,128)S(1)}, f32[256,512]{1,0:T(8,128)}, u32[]{:S(2)}, u32[]{:S(2)}) collective-permute-start(f32[256,512]{1,0:T(8,128)S(1)} %fusion.5), channel_id=1, source_target_pairs={} | collective-permute-start | bytes 1572872 | tf_op jit(solution)/shard_map/ppermute | solution.py:37
  3.8 29.9 %collective-permute-start.1 = (f32[256,512]{1,0:T(8,128)S(1)}, f32[256,512]{1,0:T(8,128)}, u32[]{:S(2)}, u32[]{:S(2)}) collective-permute-start(f32[256,512]{1,0:T(8,128)S(1)} %fusion.5), channel_id=1, source_target_pairs={{0,3},{4,7},{8,11},{12,15},{16,19},{20,23},{24,27},{28,31}} | collective-permute-start | bytes 1572872 | tf_op jit(solution)/shard_map/ppermute | solution.py:37
  8.9 25.9 %collective-permute-start.2 = (f32[256,512]{1,0:T(8,128)S(1)}, f32[256,512]{1,0:T(8,128)}, u32[]{:S(2)}, u32[]{:S(2)}) collective-permute-start(f32[256,512]{1,0:T(8,128)S(1)} %fusion.5), channel_id=1, source_target_pairs={{0,2},{1,3},{4,6},{5,7},{8,10},{9,11},{12,14},{13,15},{16,18},{17,... | collective-permute-start | bytes 1572872 | tf_op jit(solution)/shard_map/ppermute | solution.py:37
  11.0 24.9 %collective-permute-start.3 = (f32[256,512]{1,0:T(8,128)S(1)}, f32[256,512]{1,0:T(8,128)}, u32[]{:S(2)}, u32[]{:S(2)}) collective-permute-start(f32[256,512]{1,0:T(8,128)S(1)} %fusion.5), channel_id=1, source_target_pairs={{0,1},{1,2},{2,3},{4,5},{5,6},{6,7},{8,9},{9,10},{10,11},{12,13},{... | collective-permute-start | bytes 1572872 | tf_op jit(solution)/shard_map/ppermute | solution.py:37
  41.7 138.2 %copy-start.8 = (s32[2048]{0:T(1024)S(1)}, s32[2048]{0:T(1024)}, u32[]{:S(2)}) copy-start(s32[2048]{0:T(1024)} %param.11) | copy-start | bytes 24580
  131.1 10.2 %collective-permute-start.4 = (bf16[256,512]{1,0:T(8,128)(2,1)S(1)}, bf16[256,512]{1,0:T(8,128)(2,1)S(1)}, u32[]{:S(2)}, u32[]{:S(2)}) collective-permute-start(bf16[256,512]{1,0:T(8,128)(2,1)S(1)} %bitcast.31), channel_id=1, source_target_pairs={{0,4},{4,8},{8,12},{12,16},{16,20},{20,24},{24,28},{28,0},{1,5},{5... | collective-permute-start | bytes 786440 | tf_op jit(solution)/shard_map/ppermute | solution.py:23
  141.4 9.3 %collective-permute-start.5 = (bf16[256,512]{1,0:T(8,128)(2,1)S(1)}, bf16[256,512]{1,0:T(8,128)(2,1)S(1)}, u32[]{:S(2)}, u32[]{:S(2)}) collective-permute-start(bf16[256,512]{1,0:T(8,128)(2,1)S(1)} %collective-permute-done.4), channel_id=1, source_target_pairs={{0,4},{4,8},{8,12},{12,16},{16,20},{20,24},{24,28},{28,0},{1,5},{5... | collective-permute-start | bytes 786440 | tf_op jit(solution)/shard_map/ppermute | solution.py:23
  150.7 0.7 copy-start.2
  151.4 9.1 %collective-permute-start.6 = (bf16[256,512]{1,0:T(8,128)(2,1)S(1)}, bf16[256,512]{1,0:T(8,128)(2,1)S(1)}, u32[]{:S(2)}, u32[]{:S(2)}) collective-permute-start(bf16[256,512]{1,0:T(8,128)(2,1)S(1)} %collective-permute-done.5), channel_id=1, source_target_pairs={{0,4},{4,8},{8,12},{12,16},{16,20},{20,24},{24,28},{28,0},{1,5},{5... | collective-permute-start | bytes 786440 | tf_op jit(solution)/shard_map/ppermute | solution.py:23
  160.5 0.7 copy-start.3
  161.2 9.1 %collective-permute-start.7 = (bf16[256,512]{1,0:T(8,128)(2,1)S(1)}, bf16[256,512]{1,0:T(8,128)(2,1)S(1)}, u32[]{:S(2)}, u32[]{:S(2)}) collective-permute-start(bf16[256,512]{1,0:T(8,128)(2,1)S(1)} %collective-permute-done.6), channel_id=1, source_target_pairs={{0,4},{4,8},{8,12},{12,16},{16,20},{20,24},{24,28},{28,0},{1,5},{5... | collective-permute-start | bytes 786440 | tf_op jit(solution)/shard_map/ppermute | solution.py:23
  170.2 20.3 %copy-start.4 = (bf16[256,512]{1,0:T(8,128)(2,1)}, bf16[256,512]{1,0:T(8,128)(2,1)S(1)}, u32[]{:S(2)}) copy-start(bf16[256,512]{1,0:T(8,128)(2,1)S(1)} %collective-permute-done.7) | copy-start | bytes 786436
  170.2 9.7 %collective-permute-start.8 = (bf16[256,512]{1,0:T(8,128)(2,1)S(1)}, bf16[256,512]{1,0:T(8,128)(2,1)S(1)}, u32[]{:S(2)}, u32[]{:S(2)}) collective-permute-start(bf16[256,512]{1,0:T(8,128)(2,1)S(1)} %collective-permute-done.7), channel_id=1, source_target_pairs={{0,4},{4,8},{8,12},{12,16},{16,20},{20,24},{24,28},{28,0},{1,5},{5... | collective-permute-start | bytes 786440 | tf_op jit(solution)/shard_map/ppermute | solution.py:23
  179.9 10.6 %copy-start.6 = (bf16[256,512]{1,0:T(8,128)(2,1)}, bf16[256,512]{1,0:T(8,128)(2,1)S(1)}, u32[]{:S(2)}) copy-start(bf16[256,512]{1,0:T(8,128)(2,1)S(1)} %collective-permute-done.8) | copy-start | bytes 786436
  179.9 10.6 %collective-permute-start.9 = (bf16[256,512]{1,0:T(8,128)(2,1)S(1)}, bf16[256,512]{1,0:T(8,128)(2,1)}, u32[]{:S(2)}, u32[]{:S(2)}) collective-permute-start(bf16[256,512]{1,0:T(8,128)(2,1)S(1)} %collective-permute-done.8), channel_id=1, source_target_pairs={{0,4},{4,8},{8,12},{12,16},{16,20},{20,24},{24,28},{28,0},{1,5},{5... | collective-permute-start | bytes 786440 | tf_op jit(solution)/shard_map/ppermute | solution.py:23
  190.5 19.1 %collective-permute-start.10 = (bf16[256,512]{1,0:T(8,128)(2,1)}, bf16[256,512]{1,0:T(8,128)(2,1)}, u32[]{:S(2)}, u32[]{:S(2)}) collective-permute-start(bf16[256,512]{1,0:T(8,128)(2,1)} %collective-permute-done.9), channel_id=1, source_target_pairs={{0,4},{4,8},{8,12},{12,16},{16,20},{20,24},{24,28},{28,0},{1,5},{5... | collective-permute-start | bytes 786440 | tf_op jit(solution)/shard_map/ppermute | solution.py:23
  200.6 5.0 %copy-start.5 = (bf16[256,512]{1,0:T(8,128)(2,1)S(1)}, bf16[256,512]{1,0:T(8,128)(2,1)}, u32[]{:S(2)}) copy-start(bf16[256,512]{1,0:T(8,128)(2,1)} %copy-done.4) | copy-start | bytes 786436
  200.6 6.0 %copy-start.7 = (bf16[256,512]{1,0:T(8,128)(2,1)S(1)}, bf16[256,512]{1,0:T(8,128)(2,1)}, u32[]{:S(2)}) copy-start(bf16[256,512]{1,0:T(8,128)(2,1)} %copy-done.6) | copy-start | bytes 786436
  224.7 3.7 %copy-start.1 = (bf16[2048,512]{0,1:T(8,128)(2,1)S(1)}, bf16[2048,512]{0,1:T(8,128)(2,1)}, u32[]{:S(2)}) copy-start(bf16[2048,512]{0,1:T(8,128)(2,1)} %copy.127) | copy-start | bytes 6291460
